TPU v7x, 32 devices: a whole 2x2x4 slice. The times are simulated.
32 devices in a mesh: group: 1, ctx: 32 (over z, y, x, core).
Axes of the slice: x: 2, y: 2, z: 4, core: 2. Of those that a mesh axis runs over, the one named last changes fastest.
Arguments:
- history: bfloat16 [2, 1024, 8192], P('group', 'ctx'), may hold values from -6 to 6
- lengths: int32 [2], P('group'), may hold values from 256 to 1024
- token_ids: int32 [2, 512], P('group'), may hold values from 0 to 511
- embed: bfloat16 [512, 8192], P('ctx'), may hold values from -6 to 6
- residue: float32 [16, 8192], replicated, may hold values from -0.046875 to 0.046875
- decay: float32 [16, 8192], replicated, may hold values from 0.1 to 400
- skip: float32 [8192], replicated, may hold values from 0.5 to 1.5
Outputs:
- mixed: bfloat16 [2, 512, 8192], P('group', 'ctx')
Inputs may be any that keep to these rules, and one draw needn't show every extreme that they name: `lengths`: history positions at or past a sequence's length are ignored.
All inputs are finite; a program needn't handle non-finite values.
Results may differ from a plain program's by a relative error of at most 0.0005.
Values may be sent and summed in bfloat16 or wider, within the bound.
No kernel may reach another device: no remote copies, remote signals or barrier semaphores. Data moves between devices by JAX's collectives and lax.ppermute only.
A program may use at most 128 MiB of HBM per device.

v0:
```python
import jax
import jax.numpy as jnp
from jax import lax
from jax.sharding import PartitionSpec as P

STEP_LEN = 128


def body(history, lengths, token_ids, embed, residue, decay, skip):
    devices = lax.axis_size("ctx")
    myself = lax.axis_index("ctx")
    seqs, tile, width = history.shape
    narrow = width // devices
    total_len = tile * devices
    rates = decay / total_len
    start = myself * tile
    places = start + jnp.arange(tile, dtype=jnp.int32)
    inside = places[None, :] < lengths[:, None]
    masked = jnp.where(inside[:, :, None], history, jnp.zeros_like(history))
    ends = start + tile
    lift = jnp.maximum(lengths - ends, -tile).astype(jnp.float32)
    spans = (ends - places).astype(jnp.float32)

    def per_mode(rate_row):
        local = jnp.exp(-rate_row[None, :] * spans[:, None])
        part = jnp.sum(local[None, :, :] * masked, axis=1)
        return part * jnp.exp(-rate_row[None, :] * lift[:, None])

    partial_states = lax.map(per_mode, rates)
    summed = lax.psum(partial_states, "ctx")
    mine = lax.dynamic_slice_in_dim(summed, myself * narrow, narrow, 2)
    full_table = lax.all_gather(embed, "ctx", axis=0, tiled=True)
    columns = lax.dynamic_slice_in_dim(full_table, myself * narrow, narrow, 1)
    vocab = columns.shape[0]
    onehot = (token_ids[:, :, None] == jnp.arange(vocab, dtype=jnp.int32)[None, None, :]).astype(
        jnp.bfloat16
    )
    fresh = jnp.einsum("btv,vc->btc", onehot, columns, preferred_element_type=jnp.float32).astype(
        jnp.bfloat16
    )
    my_rates = lax.dynamic_slice_in_dim(rates, myself * narrow, narrow, 1)
    my_residue = lax.dynamic_slice_in_dim(residue, myself * narrow, narrow, 1)
    my_skip = lax.dynamic_slice_in_dim(skip, myself * narrow, narrow, 0)
    generated = token_ids.shape[1]
    steps_count = generated // STEP_LEN
    times = jnp.arange(generated, dtype=jnp.int32).astype(jnp.float32)
    decays = jnp.exp(-my_rates[:, None, :] * times[None, :, None])
    weighted = my_residue[:, None, :] * decays
    history_part = jnp.einsum("ktc,kbc->btc", weighted, mine, precision=lax.Precision.HIGHEST)
    fresh_wide = fresh.astype(jnp.float32)
    pieces = fresh_wide.reshape(seqs, steps_count, STEP_LEN, narrow)
    ladder = jnp.arange(STEP_LEN, dtype=jnp.int32)
    offset = ladder[:, None] - ladder[None, :]
    below = (offset >= 0)[:, :, None]
    gaps = jnp.maximum(offset, 0).astype(jnp.float32)

    def add_mode(index, block):
        rate_row = my_rates[index]
        return block + my_residue[index][None, None, :] * jnp.exp(
            -rate_row[None, None, :] * gaps[:, :, None]
        )

    toeplitz = lax.fori_loop(
        0, my_rates.shape[0], add_mode, jnp.zeros((STEP_LEN, STEP_LEN, narrow), jnp.float32)
    )
    toeplitz = jnp.where(below, toeplitz, 0.0)
    near_part = jnp.einsum("tsc,bjsc->bjtc", toeplitz, pieces, precision=lax.Precision.HIGHEST)
    ladder_f = ladder.astype(jnp.float32)
    into_step = my_residue[:, None, :] * jnp.exp(-my_rates[:, None, :] * ladder_f[None, :, None])
    out_of_step = jnp.exp(-my_rates[:, None, :] * (STEP_LEN - ladder_f)[None, :, None])
    step_decay = jnp.exp(-my_rates * STEP_LEN)
    carry = jnp.zeros((my_rates.shape[0], seqs, narrow), jnp.float32)
    far_blocks = []
    for index in range(steps_count):
        far_blocks.append(
            jnp.einsum("kuc,kbc->buc", into_step, carry, precision=lax.Precision.HIGHEST)
        )
        step_state = jnp.einsum(
            "ksc,bsc->kbc", out_of_step, pieces[:, index], precision=lax.Precision.HIGHEST
        )
        carry = step_decay[:, None, :] * carry + step_state
    far_part = jnp.stack(far_blocks, axis=1)
    conv_part = (near_part + far_part).reshape(seqs, generated, narrow)
    mixed = (history_part + conv_part + my_skip[None, None, :] * fresh_wide).astype(jnp.bfloat16)
    return lax.all_to_all(mixed, "ctx", split_axis=1, concat_axis=2, tiled=True)


def solution(mesh):
    placed = (P("group", "ctx", None), P("group"), P("group", None), P("ctx", None), P(), P(), P())
    return jax.shard_map(
        body, mesh=mesh, in_specs=placed, out_specs=P("group", "ctx", None), check_vma=False
    )
```

profile of v0, /device:TPU:0, one launch (start us, length us, event | category | flops | bytes accessed | tf_op | source)
XLA Modules:
  0.0 337.1 jit_solution(2049569387925838529)
XLA Ops:
  6.5 0.7 all-gather.2.cloned.1.call-update
  7.3 1.1 broadcast_multiply_fusion
  8.4 0.7 broadcast_compare_fusion
  9.1 0.7 maximum_convert_fusion.1
  9.8 1.4 broadcast_select_fusion
  11.2 12.9 %while.25 = (s32[]{:T(128)}, f32[16,2,8192]{2,1,0:T(2,128)S(1)}, f32[16,8192]{1,0:T(8,128)S(1)}, bf16[2,32,8192]{2,1,0:T(8,128)(2,1)S(1)}, f32[2]{0:T(128)S(1)}, /*index=5*/s32[]{:T(128)}, s32[]{:T(128)}, s32[]{:T(128)}) while((s32[]{:T(128)}, f32[16,2,8192]{2,1,0:T(2,128)S(1)}, f32[16,8192]{1,0:T(8,128)S(1)}, ...), condition=%wide.region_2.3_spmd.clone, body=%wide.region_0.2_spmd.clone.sunk | while | flops 1859682 | bytes 3474285 | solution.py:29
  11.5 0.4 multiply_reduce_fusion.2
  12.3 0.4 multiply_reduce_fusion.2
  13.1 0.4 multiply_reduce_fusion.2
  13.9 0.4 multiply_reduce_fusion.2
  14.7 0.4 multiply_reduce_fusion.2
  24.1 7.8 %copy.64 = f32[16,2,8192]{0,1,2:T(2,128)} copy(f32[16,2,8192]{2,1,0:T(2,128)S(1)} %get-tuple-element.131) | data formatting | bytes 2097152 | tf_op jit(solution)/shard_map/while | solution.py:29
  32.1 196.6 %while.26 = (s32[]{:T(128)}, f32[128,128,256]{2,1,0:T(8,128)}, f32[16,256]{1,0:T(8,128)S(1)}, f32[16,256]{1,0:T(8,128)S(1)}, s32[]{:T(128)}, /*index=5*/s32[]{:T(128)}) while((s32[]{:T(128)}, f32[128,128,256]{2,1,0:T(8,128)}, f32[16,256]{1,0:T(8,128)S(1)}, f32[16,256]{1,0:T(8,128)S(1)}, s32[]{:T(128)}, /*index=5*/s32[]{:T(128)}) %tuple.55), condition=%wide.region_5.6_spmd.clone, body=%wide.region_4.5_spmd.clone.sunk | while | flops 16826628 | bytes 33691736 | solution.py:63
  32.2 7.0 %select_add_fusion.2 = f32[128,128,256]{2,1,0:T(8,128)} fusion(f32[128,128,256]{2,1,0:T(8,128)} %get-tuple-element.278, f32[128,128]{1,0:T(8,128)S(1)} %maximum_convert_fusion.3, f32[256]{0:T(256)S(1)} %bitcast.86, f32[256]{0:T(256)S(1)} %bitcast.87, pred[]{:T(512)S(6)} %compare.3), kind=kLoop, calls=%fused_computation.8.clone.1 | loop fusion | flops 16777216 | bytes 33622016 | tf_op jit(solution)/shard_map/while/body/eval_jaxpr/add | solution.py:59
  39.3 12.5 %select_add_fusion.2 = f32[128,128,256]{2,1,0:T(8,128)} fusion(f32[128,128,256]{2,1,0:T(8,128)} %get-tuple-element.278, f32[128,128]{1,0:T(8,128)S(1)} %maximum_convert_fusion.3, f32[256]{0:T(256)S(1)} %bitcast.86, f32[256]{0:T(256)S(1)} %bitcast.87, pred[]{:T(512)S(6)} %compare.3), kind=kLoop, calls=%fused_computation.8.clone.1 | loop fusion | flops 16777216 | bytes 33622016 | tf_op jit(solution)/shard_map/while/body/eval_jaxpr/add | solution.py:59
  51.8 12.8 %select_add_fusion.2 = f32[128,128,256]{2,1,0:T(8,128)} fusion(f32[128,128,256]{2,1,0:T(8,128)} %get-tuple-element.278, f32[128,128]{1,0:T(8,128)S(1)} %maximum_convert_fusion.3, f32[256]{0:T(256)S(1)} %bitcast.86, f32[256]{0:T(256)S(1)} %bitcast.87, pred[]{:T(512)S(6)} %compare.3), kind=kLoop, calls=%fused_computation.8.clone.1 | loop fusion | flops 16777216 | bytes 33622016 | tf_op jit(solution)/shard_map/while/body/eval_jaxpr/add | solution.py:59
  64.6 12.5 %select_add_fusion.2 = f32[128,128,256]{2,1,0:T(8,128)} fusion(f32[128,128,256]{2,1,0:T(8,128)} %get-tuple-element.278, f32[128,128]{1,0:T(8,128)S(1)} %maximum_convert_fusion.3, f32[256]{0:T(256)S(1)} %bitcast.86, f32[256]{0:T(256)S(1)} %bitcast.87, pred[]{:T(512)S(6)} %compare.3), kind=kLoop, calls=%fused_computation.8.clone.1 | loop fusion | flops 16777216 | bytes 33622016 | tf_op jit(solution)/shard_map/while/body/eval_jaxpr/add | solution.py:59
  77.2 12.7 %select_add_fusion.2 = f32[128,128,256]{2,1,0:T(8,128)} fusion(f32[128,128,256]{2,1,0:T(8,128)} %get-tuple-element.278, f32[128,128]{1,0:T(8,128)S(1)} %maximum_convert_fusion.3, f32[256]{0:T(256)S(1)} %bitcast.86, f32[256]{0:T(256)S(1)} %bitcast.87, pred[]{:T(512)S(6)} %compare.3), kind=kLoop, calls=%fused_computation.8.clone.1 | loop fusion | flops 16777216 | bytes 33622016 | tf_op jit(solution)/shard_map/while/body/eval_jaxpr/add | solution.py:59
  89.9 12.8 %select_add_fusion.2 = f32[128,128,256]{2,1,0:T(8,128)} fusion(f32[128,128,256]{2,1,0:T(8,128)} %get-tuple-element.278, f32[128,128]{1,0:T(8,128)S(1)} %maximum_convert_fusion.3, f32[256]{0:T(256)S(1)} %bitcast.86, f32[256]{0:T(256)S(1)} %bitcast.87, pred[]{:T(512)S(6)} %compare.3), kind=kLoop, calls=%fused_computation.8.clone.1 | loop fusion | flops 16777216 | bytes 33622016 | tf_op jit(solution)/shard_map/while/body/eval_jaxpr/add | solution.py:59
  102.7 12.6 %select_add_fusion.2 = f32[128,128,256]{2,1,0:T(8,128)} fusion(f32[128,128,256]{2,1,0:T(8,128)} %get-tuple-element.278, f32[128,128]{1,0:T(8,128)S(1)} %maximum_convert_fusion.3, f32[256]{0:T(256)S(1)} %bitcast.86, f32[256]{0:T(256)S(1)} %bitcast.87, pred[]{:T(512)S(6)} %compare.3), kind=kLoop, calls=%fused_computation.8.clone.1 | loop fusion | flops 16777216 | bytes 33622016 | tf_op jit(solution)/shard_map/while/body/eval_jaxpr/add | solution.py:59
  115.4 12.7 %select_add_fusion.2 = f32[128,128,256]{2,1,0:T(8,128)} fusion(f32[128,128,256]{2,1,0:T(8,128)} %get-tuple-element.278, f32[128,128]{1,0:T(8,128)S(1)} %maximum_convert_fusion.3, f32[256]{0:T(256)S(1)} %bitcast.86, f32[256]{0:T(256)S(1)} %bitcast.87, pred[]{:T(512)S(6)} %compare.3), kind=kLoop, calls=%fused_computation.8.clone.1 | loop fusion | flops 16777216 | bytes 33622016 | tf_op jit(solution)/shard_map/while/body/eval_jaxpr/add | solution.py:59
  128.1 12.6 %select_add_fusion.2 = f32[128,128,256]{2,1,0:T(8,128)} fusion(f32[128,128,256]{2,1,0:T(8,128)} %get-tuple-element.278, f32[128,128]{1,0:T(8,128)S(1)} %maximum_convert_fusion.3, f32[256]{0:T(256)S(1)} %bitcast.86, f32[256]{0:T(256)S(1)} %bitcast.87, pred[]{:T(512)S(6)} %compare.3), kind=kLoop, calls=%fused_computation.8.clone.1 | loop fusion | flops 16777216 | bytes 33622016 | tf_op jit(solution)/shard_map/while/body/eval_jaxpr/add | solution.py:59
  140.8 12.5 %select_add_fusion.2 = f32[128,128,256]{2,1,0:T(8,128)} fusion(f32[128,128,256]{2,1,0:T(8,128)} %get-tuple-element.278, f32[128,128]{1,0:T(8,128)S(1)} %maximum_convert_fusion.3, f32[256]{0:T(256)S(1)} %bitcast.86, f32[256]{0:T(256)S(1)} %bitcast.87, pred[]{:T(512)S(6)} %compare.3), kind=kLoop, calls=%fused_computation.8.clone.1 | loop fusion | flops 16777216 | bytes 33622016 | tf_op jit(solution)/shard_map/while/body/eval_jaxpr/add | solution.py:59
  153.4 12.5 %select_add_fusion.2 = f32[128,128,256]{2,1,0:T(8,128)} fusion(f32[128,128,256]{2,1,0:T(8,128)} %get-tuple-element.278, f32[128,128]{1,0:T(8,128)S(1)} %maximum_convert_fusion.3, f32[256]{0:T(256)S(1)} %bitcast.86, f32[256]{0:T(256)S(1)} %bitcast.87, pred[]{:T(512)S(6)} %compare.3), kind=kLoop, calls=%fused_computation.8.clone.1 | loop fusion | flops 16777216 | bytes 33622016 | tf_op jit(solution)/shard_map/while/body/eval_jaxpr/add | solution.py:59
  166.0 12.5 %select_add_fusion.2 = f32[128,128,256]{2,1,0:T(8,128)} fusion(f32[128,128,256]{2,1,0:T(8,128)} %get-tuple-element.278, f32[128,128]{1,0:T(8,128)S(1)} %maximum_convert_fusion.3, f32[256]{0:T(256)S(1)} %bitcast.86, f32[256]{0:T(256)S(1)} %bitcast.87, pred[]{:T(512)S(6)} %compare.3), kind=kLoop, calls=%fused_computation.8.clone.1 | loop fusion | flops 16777216 | bytes 33622016 | tf_op jit(solution)/shard_map/while/body/eval_jaxpr/add | solution.py:59
  178.5 12.6 %select_add_fusion.2 = f32[128,128,256]{2,1,0:T(8,128)} fusion(f32[128,128,256]{2,1,0:T(8,128)} %get-tuple-element.278, f32[128,128]{1,0:T(8,128)S(1)} %maximum_convert_fusion.3, f32[256]{0:T(256)S(1)} %bitcast.86, f32[256]{0:T(256)S(1)} %bitcast.87, pred[]{:T(512)S(6)} %compare.3), kind=kLoop, calls=%fused_computation.8.clone.1 | loop fusion | flops 16777216 | bytes 33622016 | tf_op jit(solution)/shard_map/while/body/eval_jaxpr/add | solution.py:59
  191.1 12.4 %select_add_fusion.2 = f32[128,128,256]{2,1,0:T(8,128)} fusion(f32[128,128,256]{2,1,0:T(8,128)} %get-tuple-element.278, f32[128,128]{1,0:T(8,128)S(1)} %maximum_convert_fusion.3, f32[256]{0:T(256)S(1)} %bitcast.86, f32[256]{0:T(256)S(1)} %bitcast.87, pred[]{:T(512)S(6)} %compare.3), kind=kLoop, calls=%fused_computation.8.clone.1 | loop fusion | flops 16777216 | bytes 33622016 | tf_op jit(solution)/shard_map/while/body/eval_jaxpr/add | solution.py:59
  203.6 12.7 %select_add_fusion.2 = f32[128,128,256]{2,1,0:T(8,128)} fusion(f32[128,128,256]{2,1,0:T(8,128)} %get-tuple-element.278, f32[128,128]{1,0:T(8,128)S(1)} %maximum_convert_fusion.3, f32[256]{0:T(256)S(1)} %bitcast.86, f32[256]{0:T(256)S(1)} %bitcast.87, pred[]{:T(512)S(6)} %compare.3), kind=kLoop, calls=%fused_computation.8.clone.1 | loop fusion | flops 16777216 | bytes 33622016 | tf_op jit(solution)/shard_map/while/body/eval_jaxpr/add | solution.py:59
  216.3 12.5 %select_add_fusion.2 = f32[128,128,256]{2,1,0:T(8,128)} fusion(f32[128,128,256]{2,1,0:T(8,128)} %get-tuple-element.278, f32[128,128]{1,0:T(8,128)S(1)} %maximum_convert_fusion.3, f32[256]{0:T(256)S(1)} %bitcast.86, f32[256]{0:T(256)S(1)} %bitcast.87, pred[]{:T(512)S(6)} %compare.3), kind=kLoop, calls=%fused_computation.8.clone.1 | loop fusion | flops 16777216 | bytes 33622016 | tf_op jit(solution)/shard_map/while/body/eval_jaxpr/add | solution.py:59
  228.7 13.4 %select_bitcast_fusion = f32[128,128,256,1]{2,1,0,3:T(8,128)} fusion(f32[128,128,256]{2,1,0:T(8,128)} %get-tuple-element.132, pred[128,128]{1,0:T(8,128)(4,1)S(1)} %subtract_compare_fusion), kind=kLoop, calls=%fused_computation.12 | loop fusion | flops 4194304 | bytes 33570816 | tf_op jit(solution)/shard_map/jit(_where)/select_n | solution.py:66
  242.2 18.1 %copy.80 = f32[128,128,256,1]{1,0,3,2:T(8,128)} copy(f32[128,128,256,1]{2,1,0,3:T(8,128)} %select_bitcast_fusion) | data formatting | bytes 33554432 | tf_op jit(solution)/shard_map/jit(_where)/select_n | solution.py:66
  260.6 0.8 dynamic_slice.37
  261.3 2.8 fusion.18
  264.2 1.5 fusion.19
  265.7 0.5 copy.67
  266.5 0.6 fusion.65
  267.3 2.2 fusion.34
  269.6 2.8 fusion.17
  272.4 2.2 fusion.36
  274.6 2.8 fusion.16
  277.5 2.2 fusion.38
  279.7 3.0 fusion.15
  282.7 13.1 %fusion.23 = f32[2,4,128,256]{2,1,0,3:T(4,128)S(1)} fusion(bf16[2,4,128,256]{2,1,0,3:T(4,128)(2,1)S(1)} %reshape.164, f32[128,128,256,1]{1,0,3,2:T(8,128)S(1)} %copy-done.2, f32[2,1,128,256]{2,1,0,3:T(1,128)S(1)} %bitcast.85, f32[2,1,128,256]{2,1,0,3:T(1,128)S(1)} %bitcast.84, f32[2,1,128,256]{2,1,0,3:T(1,128)S(1)} %bitcast.83, ...), kind=kOutput, calls=%fused_computation.33 | convolution fusion | flops 403701760 | bytes 19398656 | tf_op jit(solution)/shard_map/tsc,bjsc->bjtc/dot_general | solution.py:67
  295.8 0.8 reshape.165
  296.7 8.1 %fusion.30 = bf16[2,512,256]{1,0,2:T(2,128)(2,1)S(1)} fusion(f32[2,512,256]{1,0,2:T(2,128)S(1)} %reshape.165, f32[512]{0:T(512)S(1)} %iota_convert_fusion, f32[16,256]{0,1:T(8,128)S(1)} %copy.66, f32[16,256]{0,1:T(8,128)S(1)} %copy.65, bf16[2,512,256]{1,0,2:T(2,128)(2,1)S(1)} %copy.67, f32[256]{0:T(256)S(1)} %dynamic_slice.37, ...), kind=kOutput, calls=%fused_computation.36 | convolution fusion | flops 55836672 | bytes 2395140 | tf_op jit(solution)/shard_map/ktc,kbc->btc/dot_general | solution.py:49
  304.8 1.0 copy.77
  305.8 23.6 %all_to_all.18 = bf16[2,512,256]{2,0,1:T(2,128)(2,1)S(1)} all-to-all(bf16[2,512,256]{2,0,1:T(2,128)(2,1)S(1)} %copy.77), channel_id=1, replica_groups=mesh['group'=1,'ctx'=32] {'ctx'}, dimensions={1} | all-to-all | bytes 1048576 | tf_op jit(solution)/shard_map/all_to_all | solution.py:85
  329.5 0.8 copy.86
  (138 shorter events, 12.3 us)
Async XLA Ops:
  6.5 25.4 %copy-start = (f32[16,8192]{1,0:T(8,128)S(1)}, f32[16,8192]{1,0:T(8,128)}, u32[]{:S(2)}) copy-start(f32[16,8192]{1,0:T(8,128)} %param.15) | copy-start | bytes 1572868
  6.5 257.6 %all-gather.2.cloned.1.call-start = ((), (), s32[]{:S(2)}) async-start(), calls=%async_computation.2 | async-start | bytes 8650752 | tf_op jit(solution)/shard_map/all_gather | solution.py:32
  7.3 289.4 %all-reduce.2.cloned.1.call-start = ((), (), s32[]{:S(2)}) async-start(), calls=%async_computation.1 | async-start | bytes 16777216 | tf_op jit(solution)/shard_map/psum | solution.py:30
  260.4 3.7 %copy-start.3 = (s32[2,512]{1,0:T(2,128)S(1)}, s32[2,512]{1,0:T(2,128)}, u32[]{:S(2)}) copy-start(s32[2,512]{1,0:T(2,128)} %param.13) | copy-start | bytes 12292
  269.6 13.2 %copy-start.2 = (f32[128,128,256,1]{1,0,3,2:T(8,128)S(1)}, f32[128,128,256,1]{1,0,3,2:T(8,128)}, u32[]{:S(2)}) copy-start(f32[128,128,256,1]{1,0,3,2:T(8,128)} %copy.80) | copy-start | bytes 50331652
  296.7 33.6 %copy-start.1 = (f32[16,8192]{1,0:T(8,128)S(1)}, f32[16,8192]{1,0:T(8,128)}, u32[]{:S(2)}) copy-start(f32[16,8192]{1,0:T(8,128)} %param.15) | copy-start | bytes 1572868
Sparse Core Ops, SparseCore 0:
  10.2 79.7 all-gather.1
  95.7 177.6 all-reduce.1
where the time goes:
time: 338 us; the launch traced here: 337 us
  other arithmetic  226 us (67%)
  matrix products  40.8 us (12%)
  local copies, waits for them, and re-layouts  31.4 us (9%)
  blocking collectives  23.6 us (7%)
  between operations  13.7 us (4%)
    add x16, other arithmetic, add_mode(): block + my_residue[index][None, None, :] * jnp.exp(-rate_row[None, None,...  196 us
    all_to_all x1, blocking collectives, body(): return lax.all_to_all(mixed, 'ctx', split_axis=1, concat_axis=2, tiled=True)  23.6 us
    select_n x1, local copies, waits for them, and re-layouts, body(): toeplitz = jnp.where(below, toeplitz, 0.0)  18.1 us
    select_n x1, other arithmetic, body(): toeplitz = jnp.where(below, toeplitz, 0.0)  13.4 us
    dot_general x1, matrix products, body(): jnp.einsum('tsc,bjsc->bjtc', toeplitz, pieces, precision=lax.Precision.HI...  13.1 us
    dot_general x4, matrix products, body(): jnp.einsum('kuc,kbc->buc', into_step, carry, precision=lax.Precision.HIGH...  11.5 us
    dot_general x1, matrix products, body(): jnp.einsum('ktc,kbc->btc', weighted, mine, precision=lax.Precision.HIGHEST)  8.11 us
    while x1, local copies, waits for them, and re-layouts, body(): partial_states = lax.map(per_mode, rates)  7.76 us
  transfers between devices with their start and end apart: 2, of which 0 were waited for; matrix products, arithmetic and copies ran while one was open for 85% of the time, Pallas kernels for 0%

commit v1 on v0

--- a/solution.py
+++ b/solution.py
@@ -82,7 +82,10 @@
     far_part = jnp.stack(far_blocks, axis=1)
     conv_part = (near_part + far_part).reshape(seqs, generated, narrow)
     mixed = (history_part + conv_part + my_skip[None, None, :] * fresh_wide).astype(jnp.bfloat16)
-    return lax.all_to_all(mixed, "ctx", split_axis=1, concat_axis=2, tiled=True)
+    return jnp.concatenate(
+        lax.all_to_all(jnp.stack(jnp.split(mixed, lax.axis_size("ctx"), axis=1)), "ctx", 0, 0),
+        axis=2,
+    )
 
 
 def solution(mesh):

time: 338 us -> 357 us (1.056)
  local copies, waits for them, and re-layouts: 31.4 us -> 50.3 us
    another operation x0 -> x35, local copies, waits for them, and re-layouts: none -> 19.8 us  [body(): jnp.stack(jnp.split(mixed, lax.axis_size('ctx'), axis=1))]
  transfers between devices with their start and end apart: 2 -> 2, of which waited for: 0 -> 0; matrix products, arithmetic and copies ran while one was open for 85% -> 81% of each run, Pallas kernels for 0% -> 0%
where the time goes in v1:
time: 357 us; the launch traced here: 356 us
  other arithmetic  225 us (63%)
  local copies, waits for them, and re-layouts  50.3 us (14%)
  matrix products  40.7 us (11%)
  blocking collectives  24.3 us (7%)
  between operations  14 us (4%)
    add x16, other arithmetic, add_mode(): block + my_residue[index][None, None, :] * jnp.exp(-rate_row[None, None,...  195 us
    all_to_all x1, blocking collectives, body(): lax.all_to_all(jnp.stack(jnp.split(mixed, lax.axis_size('ctx'), axis=1)),...  24.3 us
    another operation x35, local copies, waits for them, and re-layouts, body(): jnp.stack(jnp.split(mixed, lax.axis_size('ctx'), axis=1))  19.8 us
    select_n x1, local copies, waits for them, and re-layouts, body(): toeplitz = jnp.where(below, toeplitz, 0.0)  18.2 us
    select_n x1, other arithmetic, body(): toeplitz = jnp.where(below, toeplitz, 0.0)  13.1 us
    dot_general x1, matrix products, body(): jnp.einsum('tsc,bjsc->bjtc', toeplitz, pieces, precision=lax.Precision.HI...  13.1 us
    dot_general x4, matrix products, body(): jnp.einsum('kuc,kbc->buc', into_step, carry, precision=lax.Precision.HIGH...  11.5 us
    dot_general x1, matrix products, body(): jnp.einsum('ktc,kbc->btc', weighted, mine, precision=lax.Precision.HIGHEST)  8.05 us
  transfers between devices with their start and end apart: 2, of which 0 were waited for; matrix products, arithmetic and copies ran while one was open for 81% of the time, Pallas kernels for 0%

profile of v1, /device:TPU:0, one launch (start us, length us, event | category | flops | bytes accessed | tf_op | source)
XLA Modules:
  0.0 356.2 jit_solution(10829059138405149583)
XLA Ops:
  7.3 1.1 broadcast_multiply_fusion
  8.4 0.7 broadcast_compare_fusion
  9.8 1.4 broadcast_select_fusion
  11.2 12.9 %while.25 = (s32[]{:T(128)}, f32[16,2,8192]{2,1,0:T(2,128)S(1)}, f32[16,8192]{1,0:T(8,128)S(1)}, bf16[2,32,8192]{2,1,0:T(8,128)(2,1)S(1)}, f32[2]{0:T(128)S(1)}, /*index=5*/s32[]{:T(128)}, s32[]{:T(128)}, s32[]{:T(128)}) while((s32[]{:T(128)}, f32[16,2,8192]{2,1,0:T(2,128)S(1)}, f32[16,8192]{1,0:T(8,128)S(1)}, ...), condition=%wide.region_2.3_spmd.clone, body=%wide.region_0.2_spmd.clone.sunk | while | flops 1859682 | bytes 3474285 | solution.py:29
  24.1 7.7 %copy.78 = f32[16,2,8192]{0,1,2:T(2,128)} copy(f32[16,2,8192]{2,1,0:T(2,128)S(1)} %get-tuple-element.131) | data formatting | bytes 2097152 | tf_op jit(solution)/shard_map/while | solution.py:29
  32.1 196.2 %while.26 = (s32[]{:T(128)}, f32[128,128,256]{2,1,0:T(8,128)}, f32[16,256]{1,0:T(8,128)S(1)}, f32[16,256]{1,0:T(8,128)S(1)}, s32[]{:T(128)}, /*index=5*/s32[]{:T(128)}) while((s32[]{:T(128)}, f32[128,128,256]{2,1,0:T(8,128)}, f32[16,256]{1,0:T(8,128)S(1)}, f32[16,256]{1,0:T(8,128)S(1)}, s32[]{:T(128)}, /*index=5*/s32[]{:T(128)}) %tuple.85), condition=%wide.region_5.6_spmd.clone, body=%wide.region_4.5_spmd.clone.sunk | while | flops 16826628 | bytes 33691736 | solution.py:63
  32.1 7.0 %select_add_fusion.2 = f32[128,128,256]{2,1,0:T(8,128)} fusion(f32[128,128,256]{2,1,0:T(8,128)} %get-tuple-element.310, f32[128,128]{1,0:T(8,128)S(1)} %maximum_convert_fusion.3, f32[256]{0:T(256)S(1)} %bitcast.148, f32[256]{0:T(256)S(1)} %bitcast.149, pred[]{:T(512)S(6)} %compare.3), kind=kLoop, calls=%fused_computation.8.clone.1 | loop fusion | flops 16777216 | bytes 33622016 | tf_op jit(solution)/shard_map/while/body/eval_jaxpr/add | solution.py:59
  39.2 12.4 %select_add_fusion.2 = f32[128,128,256]{2,1,0:T(8,128)} fusion(f32[128,128,256]{2,1,0:T(8,128)} %get-tuple-element.310, f32[128,128]{1,0:T(8,128)S(1)} %maximum_convert_fusion.3, f32[256]{0:T(256)S(1)} %bitcast.148, f32[256]{0:T(256)S(1)} %bitcast.149, pred[]{:T(512)S(6)} %compare.3), kind=kLoop, calls=%fused_computation.8.clone.1 | loop fusion | flops 16777216 | bytes 33622016 | tf_op jit(solution)/shard_map/while/body/eval_jaxpr/add | solution.py:59
  51.6 12.7 %select_add_fusion.2 = f32[128,128,256]{2,1,0:T(8,128)} fusion(f32[128,128,256]{2,1,0:T(8,128)} %get-tuple-element.310, f32[128,128]{1,0:T(8,128)S(1)} %maximum_convert_fusion.3, f32[256]{0:T(256)S(1)} %bitcast.148, f32[256]{0:T(256)S(1)} %bitcast.149, pred[]{:T(512)S(6)} %compare.3), kind=kLoop, calls=%fused_computation.8.clone.1 | loop fusion | flops 16777216 | bytes 33622016 | tf_op jit(solution)/shard_map/while/body/eval_jaxpr/add | solution.py:59
  64.4 12.5 %select_add_fusion.2 = f32[128,128,256]{2,1,0:T(8,128)} fusion(f32[128,128,256]{2,1,0:T(8,128)} %get-tuple-element.310, f32[128,128]{1,0:T(8,128)S(1)} %maximum_convert_fusion.3, f32[256]{0:T(256)S(1)} %bitcast.148, f32[256]{0:T(256)S(1)} %bitcast.149, pred[]{:T(512)S(6)} %compare.3), kind=kLoop, calls=%fused_computation.8.clone.1 | loop fusion | flops 16777216 | bytes 33622016 | tf_op jit(solution)/shard_map/while/body/eval_jaxpr/add | solution.py:59
  76.9 12.6 %select_add_fusion.2 = f32[128,128,256]{2,1,0:T(8,128)} fusion(f32[128,128,256]{2,1,0:T(8,128)} %get-tuple-element.310, f32[128,128]{1,0:T(8,128)S(1)} %maximum_convert_fusion.3, f32[256]{0:T(256)S(1)} %bitcast.148, f32[256]{0:T(256)S(1)} %bitcast.149, pred[]{:T(512)S(6)} %compare.3), kind=kLoop, calls=%fused_computation.8.clone.1 | loop fusion | flops 16777216 | bytes 33622016 | tf_op jit(solution)/shard_map/while/body/eval_jaxpr/add | solution.py:59
  89.6 13.0 %select_add_fusion.2 = f32[128,128,256]{2,1,0:T(8,128)} fusion(f32[128,128,256]{2,1,0:T(8,128)} %get-tuple-element.310, f32[128,128]{1,0:T(8,128)S(1)} %maximum_convert_fusion.3, f32[256]{0:T(256)S(1)} %bitcast.148, f32[256]{0:T(256)S(1)} %bitcast.149, pred[]{:T(512)S(6)} %compare.3), kind=kLoop, calls=%fused_computation.8.clone.1 | loop fusion | flops 16777216 | bytes 33622016 | tf_op jit(solution)/shard_map/while/body/eval_jaxpr/add | solution.py:59
  102.6 12.5 %select_add_fusion.2 = f32[128,128,256]{2,1,0:T(8,128)} fusion(f32[128,128,256]{2,1,0:T(8,128)} %get-tuple-element.310, f32[128,128]{1,0:T(8,128)S(1)} %maximum_convert_fusion.3, f32[256]{0:T(256)S(1)} %bitcast.148, f32[256]{0:T(256)S(1)} %bitcast.149, pred[]{:T(512)S(6)} %compare.3), kind=kLoop, calls=%fused_computation.8.clone.1 | loop fusion | flops 16777216 | bytes 33622016 | tf_op jit(solution)/shard_map/while/body/eval_jaxpr/add | solution.py:59
  115.2 12.6 %select_add_fusion.2 = f32[128,128,256]{2,1,0:T(8,128)} fusion(f32[128,128,256]{2,1,0:T(8,128)} %get-tuple-element.310, f32[128,128]{1,0:T(8,128)S(1)} %maximum_convert_fusion.3, f32[256]{0:T(256)S(1)} %bitcast.148, f32[256]{0:T(256)S(1)} %bitcast.149, pred[]{:T(512)S(6)} %compare.3), kind=kLoop, calls=%fused_computation.8.clone.1 | loop fusion | flops 16777216 | bytes 33622016 | tf_op jit(solution)/shard_map/while/body/eval_jaxpr/add | solution.py:59
  127.8 12.6 %select_add_fusion.2 = f32[128,128,256]{2,1,0:T(8,128)} fusion(f32[128,128,256]{2,1,0:T(8,128)} %get-tuple-element.310, f32[128,128]{1,0:T(8,128)S(1)} %maximum_convert_fusion.3, f32[256]{0:T(256)S(1)} %bitcast.148, f32[256]{0:T(256)S(1)} %bitcast.149, pred[]{:T(512)S(6)} %compare.3), kind=kLoop, calls=%fused_computation.8.clone.1 | loop fusion | flops 16777216 | bytes 33622016 | tf_op jit(solution)/shard_map/while/body/eval_jaxpr/add | solution.py:59
  140.5 12.5 %select_add_fusion.2 = f32[128,128,256]{2,1,0:T(8,128)} fusion(f32[128,128,256]{2,1,0:T(8,128)} %get-tuple-element.310, f32[128,128]{1,0:T(8,128)S(1)} %maximum_convert_fusion.3, f32[256]{0:T(256)S(1)} %bitcast.148, f32[256]{0:T(256)S(1)} %bitcast.149, pred[]{:T(512)S(6)} %compare.3), kind=kLoop, calls=%fused_computation.8.clone.1 | loop fusion | flops 16777216 | bytes 33622016 | tf_op jit(solution)/shard_map/while/body/eval_jaxpr/add | solution.py:59
  153.1 12.5 %select_add_fusion.2 = f32[128,128,256]{2,1,0:T(8,128)} fusion(f32[128,128,256]{2,1,0:T(8,128)} %get-tuple-element.310, f32[128,128]{1,0:T(8,128)S(1)} %maximum_convert_fusion.3, f32[256]{0:T(256)S(1)} %bitcast.148, f32[256]{0:T(256)S(1)} %bitcast.149, pred[]{:T(512)S(6)} %compare.3), kind=kLoop, calls=%fused_computation.8.clone.1 | loop fusion | flops 16777216 | bytes 33622016 | tf_op jit(solution)/shard_map/while/body/eval_jaxpr/add | solution.py:59
  165.6 12.4 %select_add_fusion.2 = f32[128,128,256]{2,1,0:T(8,128)} fusion(f32[128,128,256]{2,1,0:T(8,128)} %get-tuple-element.310, f32[128,128]{1,0:T(8,128)S(1)} %maximum_convert_fusion.3, f32[256]{0:T(256)S(1)} %bitcast.148, f32[256]{0:T(256)S(1)} %bitcast.149, pred[]{:T(512)S(6)} %compare.3), kind=kLoop, calls=%fused_computation.8.clone.1 | loop fusion | flops 16777216 | bytes 33622016 | tf_op jit(solution)/shard_map/while/body/eval_jaxpr/add | solution.py:59
  178.1 12.6 %select_add_fusion.2 = f32[128,128,256]{2,1,0:T(8,128)} fusion(f32[128,128,256]{2,1,0:T(8,128)} %get-tuple-element.310, f32[128,128]{1,0:T(8,128)S(1)} %maximum_convert_fusion.3, f32[256]{0:T(256)S(1)} %bitcast.148, f32[256]{0:T(256)S(1)} %bitcast.149, pred[]{:T(512)S(6)} %compare.3), kind=kLoop, calls=%fused_computation.8.clone.1 | loop fusion | flops 16777216 | bytes 33622016 | tf_op jit(solution)/shard_map/while/body/eval_jaxpr/add | solution.py:59
  190.7 12.4 %select_add_fusion.2 = f32[128,128,256]{2,1,0:T(8,128)} fusion(f32[128,128,256]{2,1,0:T(8,128)} %get-tuple-element.310, f32[128,128]{1,0:T(8,128)S(1)} %maximum_convert_fusion.3, f32[256]{0:T(256)S(1)} %bitcast.148, f32[256]{0:T(256)S(1)} %bitcast.149, pred[]{:T(512)S(6)} %compare.3), kind=kLoop, calls=%fused_computation.8.clone.1 | loop fusion | flops 16777216 | bytes 33622016 | tf_op jit(solution)/shard_map/while/body/eval_jaxpr/add | solution.py:59
  203.1 12.6 %select_add_fusion.2 = f32[128,128,256]{2,1,0:T(8,128)} fusion(f32[128,128,256]{2,1,0:T(8,128)} %get-tuple-element.310, f32[128,128]{1,0:T(8,128)S(1)} %maximum_convert_fusion.3, f32[256]{0:T(256)S(1)} %bitcast.148, f32[256]{0:T(256)S(1)} %bitcast.149, pred[]{:T(512)S(6)} %compare.3), kind=kLoop, calls=%fused_computation.8.clone.1 | loop fusion | flops 16777216 | bytes 33622016 | tf_op jit(solution)/shard_map/while/body/eval_jaxpr/add | solution.py:59
  215.8 12.4 %select_add_fusion.2 = f32[128,128,256]{2,1,0:T(8,128)} fusion(f32[128,128,256]{2,1,0:T(8,128)} %get-tuple-element.310, f32[128,128]{1,0:T(8,128)S(1)} %maximum_convert_fusion.3, f32[256]{0:T(256)S(1)} %bitcast.148, f32[256]{0:T(256)S(1)} %bitcast.149, pred[]{:T(512)S(6)} %compare.3), kind=kLoop, calls=%fused_computation.8.clone.1 | loop fusion | flops 16777216 | bytes 33622016 | tf_op jit(solution)/shard_map/while/body/eval_jaxpr/add | solution.py:59
  228.2 13.1 %select_bitcast_fusion = f32[128,128,256,1]{2,1,0,3:T(8,128)} fusion(f32[128,128,256]{2,1,0:T(8,128)} %get-tuple-element.132, pred[128,128]{1,0:T(8,128)(4,1)S(1)} %subtract_compare_fusion), kind=kLoop, calls=%fused_computation.12 | loop fusion | flops 4194304 | bytes 33570816 | tf_op jit(solution)/shard_map/jit(_where)/select_n | solution.py:66
  241.4 18.2 %copy.124 = f32[128,128,256,1]{1,0,3,2:T(8,128)} copy(f32[128,128,256,1]{2,1,0,3:T(8,128)} %select_bitcast_fusion) | data formatting | bytes 33554432 | tf_op jit(solution)/shard_map/jit(_where)/select_n | solution.py:66
  259.9 0.8 dynamic_slice.37
  260.7 2.8 fusion.18
  263.5 1.5 fusion.19
  266.7 2.2 fusion.34
  268.9 2.8 fusion.17
  271.8 2.2 fusion.36
  274.0 2.8 fusion.16
  276.8 2.2 fusion.38
  279.0 3.0 fusion.15
  282.0 13.1 %fusion.23 = f32[2,4,128,256]{2,1,0,3:T(4,128)S(1)} fusion(bf16[2,4,128,256]{2,1,0,3:T(4,128)(2,1)S(1)} %reshape.170, f32[128,128,256,1]{1,0,3,2:T(8,128)S(1)} %copy-done.2, f32[2,1,128,256]{2,1,0,3:T(1,128)S(1)} %bitcast.147, f32[2,1,128,256]{2,1,0,3:T(1,128)S(1)} %bitcast.146, f32[2,1,128,256]{2,1,0,3:T(1,128)S(1)} %bitcast.145, ...), kind=kOutput, calls=%fused_computation.33 | convolution fusion | flops 403701760 | bytes 19398656 | tf_op jit(solution)/shard_map/tsc,bjsc->bjtc/dot_general | solution.py:67
  295.1 0.8 reshape.171
  296.0 8.0 %fusion.30 = bf16[2,512,256]{1,0,2:T(2,128)(2,1)S(1)} fusion(f32[2,512,256]{1,0,2:T(2,128)S(1)} %reshape.171, f32[512]{0:T(512)S(1)} %iota_convert_fusion, f32[16,256]{0,1:T(8,128)S(1)} %copy.80, f32[16,256]{0,1:T(8,128)S(1)} %copy.79, bf16[2,512,256]{1,0,2:T(2,128)(2,1)S(1)} %copy.81, f32[256]{0:T(256)S(1)} %dynamic_slice.37, ...), kind=kOutput, calls=%fused_computation.36 | convolution fusion | flops 55836672 | bytes 2395140 | tf_op jit(solution)/shard_map/ktc,kbc->btc/dot_general | solution.py:49
  304.0 2.5 slice_bitcast_fusion.19
  306.5 2.6 slice_bitcast_fusion
  309.2 1.6 copy.92
  310.8 1.6 copy.93
  312.4 1.6 copy.94
  314.0 1.6 copy.95
  315.6 1.6 copy.96
  317.1 1.6 copy.97
  318.7 1.6 copy.98
  320.3 1.6 copy.99
  324.3 24.3 %all_to_all.5 = bf16[32,2,16,256]{3,2,1,0:T(8,128)(2,1)S(1)} all-to-all(bf16[32,2,16,256]{3,2,1,0:T(8,128)(2,1)S(1)} %constant_dynamic-update-slice_fusion), channel_id=1, replica_groups=mesh['group'=1,'ctx'=32] {'ctx'}, dimensions={0} | all-to-all | bytes 1048576 | tf_op jit(solution)/shard_map/all_to_all | solution.py:86
  348.6 0.8 copy.130
  (218 shorter events, 18.5 us)
Async XLA Ops:
  6.5 25.4 %copy-start = (f32[16,8192]{1,0:T(8,128)S(1)}, f32[16,8192]{1,0:T(8,128)}, u32[]{:S(2)}) copy-start(f32[16,8192]{1,0:T(8,128)} %param.15) | copy-start | bytes 1572868
  6.5 257.0 %all-gather.2.cloned.1.call-start = ((), (), s32[]{:S(2)}) async-start(), calls=%async_computation.2 | async-start | bytes 8650752 | tf_op jit(solution)/shard_map/all_gather | solution.py:32
  7.3 288.7 %all-reduce.2.cloned.1.call-start = ((), (), s32[]{:S(2)}) async-start(), calls=%async_computation.1 | async-start | bytes 16777216 | tf_op jit(solution)/shard_map/psum | solution.py:30
  259.8 3.7 %copy-start.11 = (s32[2,512]{1,0:T(2,128)S(1)}, s32[2,512]{1,0:T(2,128)}, u32[]{:S(2)}) copy-start(s32[2,512]{1,0:T(2,128)} %param.13) | copy-start | bytes 12292
  268.9 13.1 %copy-start.2 = (f32[128,128,256,1]{1,0,3,2:T(8,128)S(1)}, f32[128,128,256,1]{1,0,3,2:T(8,128)}, u32[]{:S(2)}) copy-start(f32[128,128,256,1]{1,0,3,2:T(8,128)} %copy.124) | copy-start | bytes 50331652
  322.0 1.9 copy-start.9
  322.0 1.9 copy-start.8
  322.0 1.9 copy-start.7
  322.0 2.0 copy-start.6
  322.0 2.0 copy-start.5
  322.0 2.0 copy-start.4
  322.0 2.0 copy-start.3
  322.1 1.8 copy-start.10
  323.2 26.2 %copy-start.1 = (f32[16,8192]{1,0:T(8,128)S(1)}, f32[16,8192]{1,0:T(8,128)}, u32[]{:S(2)}) copy-start(f32[16,8192]{1,0:T(8,128)} %param.15) | copy-start | bytes 1572868
Sparse Core Ops, SparseCore 0:
  10.2 79.7 all-gather.1
  95.6 177.6 all-reduce.1
